TPU v7x, 256 devices: a whole 4x4x8 slice. The times are simulated.
256 devices in a mesh: band: 2 (over core), grow: 8 (over z), gcol: 16 (over y, x).
Axes of the slice: x: 4, y: 4, z: 8, core: 2. Of those that a mesh axis runs over, the one named last changes fastest.
Arguments:
- valence_orbitals: bfloat16 [16, 98304], replicated, may hold values from -6 to 6
- conduction_orbitals: bfloat16 [1024, 98304], P(('band', 'grow', 'gcol')), may hold values from -6 to 6
- valence_energy: float32 [16], replicated, may hold values from -3 to -0.5
- conduction_energy: float32 [1024], replicated, may hold values from 0.5 to 3
- coulomb_root: float32 [12288], replicated, may hold values from 0.2 to 2
- pair_bands: int32 [2, 5120], P(None, ('band', 'grow', 'gcol')), may hold values from 0 to 1023, as said below
- slot_counts: int32 [256], P(('band', 'grow', 'gcol')), may hold values from 1 to 19, as said below
Outputs:
- chi_zero: float32 [2, 12288, 12288], P('band', 'grow', 'gcol')
Inputs may be any that keep to these rules, and one draw needn't show every extreme that they name: `pair_bands`: the slots of device d name conduction orbitals d * 4 to (d + 1) * 4 - 1 only, each of them at least once; no (valence, conduction) pair appears in two slots anywhere. `slot_counts`: the two devices of one chip (same grow and gcol index, band 0 and band 1) hold at most 20 live slots together; some chip holds exactly 20, and some device holds exactly 19.
All inputs are finite; a program needn't handle non-finite values.
Results may differ from a plain program's by a relative error of at most 0.012.
Values may be sent and summed in bfloat16 or wider, within the bound.
No kernel may reach another device: no remote copies, remote signals or barrier semaphores. Data moves between devices by JAX's collectives and lax.ppermute only.
A program may use at most 128 MiB of HBM per device.

v0:
```python
import math

import jax
import jax.numpy as jnp
import numpy as np
from jax import lax
from jax.experimental import pallas as pl
from jax.experimental.pallas import tpu as pltpu
from jax.sharding import Mesh
from jax.sharding import PartitionSpec as P


N1, N2, N3 = 16, 24, 32
M1, M2, M3 = 32, 48, 64
NP = N2 * N3
KP = M2 * M3
MG = M1 * KP
ROW = 2 * NP
TOTAL = 5120
SLOTS = 20
HALF = 10
GROW, GCOL = 8, 16
LANES = 128
CHUNKS = KP // LANES
LINES = MG // LANES + 4
PANEL = GROW * GCOL * HALF
BLOCK = 64
ROWBLOCK = 120
COLROWS = GCOL * BLOCK + 4
WIDTH = NP // LANES
STEP = 512
F32, BF16 = jnp.float32, jnp.bfloat16
VMEM = pltpu.VMEM
SMEM = pltpu.SMEM


def wave_table(keep, length):
    wave = (np.arange(keep)[:, None] - keep // 2) % length
    angles = 2.0 * np.pi * (wave * np.arange(length)[None, :] % length) / length
    return np.cos(angles) + np.sin(angles)


def halves(table):
    high = table.astype(np.float32).astype(BF16)
    return high, (table - high.astype(np.float64)).astype(np.float32).astype(BF16)


def tables():
    second = np.repeat(wave_table(N2, M2).T, N3, axis=1)
    third = np.tile(wave_table(N3, M3).T, (1, N2))
    first = wave_table(N1, M1)
    mixed = np.zeros((N1, 16, HALF, M1))
    for p in range(HALF):
        mixed[:, p, p] = first
    return (
        second.astype(np.float32),
        third.astype(np.float32),
        halves(mixed.reshape(N1 * 16, HALF * M1)),
    )


def ready_kernel(source, vals, val, sems):
    count = 4
    size = MG // count
    copies = []
    for i in range(count):
        where = pl.ds(i * size, size)
        copies.append(pltpu.make_async_copy(source.at[:, where], val.at[:, where], sems.at[i]))
        copies[-1].start()
    for i, copy in enumerate(copies):
        copy.wait()

        def spread(a, carry):
            for t in range(CHUNKS):
                where = pl.ds(pl.multiple_of(a * KP + t * LANES, LANES), LANES)
                vals[pl.ds(t * M1 + a, 16, stride=LINES), :] = val[:, where].astype(F32)
            return carry

        lax.fori_loop(i * M1 // count, (i + 1) * M1 // count, spread, 0)


def ready_call(val, interpret=False):
    return pl.pallas_call(
        ready_kernel,
        out_shape=jax.ShapeDtypeStruct((16 * LINES, LANES), F32),
        in_specs=[pl.BlockSpec(memory_space=pltpu.HBM)],
        out_specs=pl.BlockSpec(memory_space=VMEM),
        scratch_shapes=[VMEM((16, MG), BF16), pltpu.SemaphoreType.DMA((4,))],
        compiler_params=pltpu.CompilerParams(vmem_limit_bytes=12 << 20),
        interpret=interpret,
        name="ready",
    )(stay(val))


def density_kernel(
    place, mine, other, my_count, other_count, vals, *refs,
):
    hbm, refs = refs[:9], refs[9:]
    col_out = refs[0]
    row_outs = refs[1:6]
    cons, lhs, acc, table_a, table_b, done, lines, row_lines = refs[6:14]
    local, sems = refs[14:23], refs[23]
    copies = [pltpu.make_async_copy(a, b, sems.at[i]) for i, (a, b) in enumerate(zip(hbm, local))]
    for copy in copies:
        copy.start()
    con_mine, con_other, second, third, mix_hi, mix_lo, scale, val_e, con_e = local
    band = place[0] >> 7
    z = (place[0] >> 4) & 7
    for copy in copies[:2]:
        copy.wait()

    def spread(a, carry):
        for t in range(CHUNKS):
            where = pl.ds(pl.multiple_of(a * KP + t * LANES, LANES), LANES)
            line = t * M1 + a
            cons[pl.ds(line, 8, stride=LINES), :] = jnp.concatenate(
                [con_mine[:, where].astype(F32), con_other[:, where].astype(F32)], 0
            )
        return carry

    lax.fori_loop(0, M1, spread, 0)
    for copy in copies[2:]:
        copy.wait()

    is_first = band == 0
    first_count = jnp.where(is_first, my_count[0], other_count[0])
    both_count = my_count[0] + other_count[0]
    lane = lax.broadcasted_iota(jnp.int32, (1, LANES), 1) & 15
    gaps = []
    for h in range(2):
        gap = jnp.ones((1, LANES), F32)
        for p in range(HALF):
            pos = h * HALF + p
            from_first = pos < first_count
            slot = jnp.minimum(jnp.where(from_first, pos, pos - first_count), SLOTS - 1)
            own = from_first == is_first
            v = jnp.where(own, mine[0, slot], other[0, slot])
            c = jnp.where(own, mine[1, slot], other[1, slot])
            gap = jnp.where(lane == p, con_e[c] - val_e[v], gap)
            v_line = v * LINES
            c_line = (jnp.where(own, 0, 4) + (c & 3)) * LINES
            top = pos * M1

            def product(t, carry):
                made = vals[pl.ds(v_line + t * M1, M1), :] * cons[pl.ds(c_line + t * M1, M1), :]
                where = pl.ds(pl.multiple_of(t * LANES, LANES), LANES)
                lhs[top : top + M1, where] = made.astype(BF16)
                return carry

            lax.fori_loop(0, CHUNKS, product, 0, unroll=6)
        gaps.append(gap)

    acc[...] = jnp.zeros_like(acc)

    def make(table, k):
        for i in range(STEP // M3):
            table[i * M3 : (i + 1) * M3, :] = (
                second[pl.ds(k * (STEP // M3) + i, 1), :] * third[...]
            ).astype(BF16)

    def add(table, k):
        where = pl.ds(pl.multiple_of(k * STEP, STEP), STEP)
        acc[...] += jnp.dot(lhs[:, where], table[...], preferred_element_type=F32)

    last = KP // STEP - 1
    make(table_a, 0)

    def transform(k, carry):
        make(table_b, 2 * k + 1)
        add(table_a, 2 * k)
        make(table_a, jnp.minimum(2 * k + 2, last))
        add(table_b, 2 * k + 1)
        return carry

    lax.fori_loop(0, KP // STEP // 2, transform, 0)
    at_lane = lax.broadcasted_iota(jnp.int32, (1, LANES), 1)
    frequency = (at_lane >> 4).astype(F32)
    norm = 1.0 / math.sqrt(MG)
    for h in range(2):
        mid = acc[h * HALF * M1 : (h + 1) * HALF * M1, :]
        mid_hi = mid.astype(BF16)
        mid_lo = (mid - mid_hi.astype(F32)).astype(BF16)
        done[...] = (
            jnp.dot(mix_hi[...], mid_hi, preferred_element_type=F32)
            + jnp.dot(mix_hi[...], mid_lo, preferred_element_type=F32)
            + jnp.dot(mix_lo[...], mid_hi, preferred_element_type=F32)
        ) * jnp.concatenate(
            [jnp.broadcast_to(scale[:, k * NP : (k + 1) * NP] * norm, (16, NP)) for k in range(N1)], 0
        )
        gap = gaps[h]
        live = (h * HALF + lane < both_count) & (lane < HALF) & (at_lane < 32)
        weight = jnp.where(
            live, 2.0 * gap / (gap * gap + frequency * frequency), 0.0
        ) * (1.0 / math.sqrt(TOTAL))
        w_hi = weight.astype(BF16).astype(F32)
        w_mid = (weight - w_hi).astype(BF16).astype(F32)
        lines[WIDTH * HALF : WIDTH * HALF + 1, :] = w_hi
        lines[WIDTH * HALF + 1 : WIDTH * HALF + 2, :] = w_mid
        lines[WIDTH * HALF + 2 : WIDTH * HALF + 3, :] = weight - w_hi - w_mid
        lines[WIDTH * HALF + 3 : WIDTH * HALF + 4, :] = jnp.zeros((1, LANES), F32)

        @pl.when(band == h)
        def _():
            for k in range(N1):
                for ch in range(WIDTH):
                    lines[ch * HALF : (ch + 1) * HALF, :] = done[
                        k * 16 : k * 16 + HALF, ch * LANES : (ch + 1) * LANES
                    ]
                col_out[k] = lines[...].astype(BF16)

        def message(step):
            target = jnp.where(band == 0, z + step, z - step + GROW) & 7
            for s in range(2):
                block = done[pl.ds(pl.multiple_of((2 * target + s) * 16, 16), 16), :]
                for ch in range(WIDTH):
                    at = (s * WIDTH + ch) * HALF
                    row_lines[at : at + HALF, :] = block[:HALF, ch * LANES : (ch + 1) * LANES]
            return row_lines[...].astype(BF16)

        for step in range(1, 4):
            row_outs[step][jnp.where(band == h, 0, 1)] = message(step)

        @pl.when(band == h)
        def _():
            row_outs[4][0] = message(4)

        @pl.when(band != h)
        def _():
            row_outs[0][0] = message(0)


def stay(array):
    return pltpu.with_memory_space_constraint(jnp.asarray(array), pltpu.HBM)


def density_call(
    place, mine, other, my_count, other_count, val_e, con_e, vals, con_mine, con_other, scale, interpret=False
):
    second, third, (mix_hi, mix_lo) = tables()
    smem = pl.BlockSpec(memory_space=SMEM)
    vmem = pl.BlockSpec(memory_space=VMEM)
    hbm = pl.BlockSpec(memory_space=pltpu.HBM)
    anywhere = pl.BlockSpec(memory_space=pl.ANY)
    return pl.pallas_call(
        density_kernel,
        out_shape=[
            jax.ShapeDtypeStruct((N1, BLOCK, LANES), BF16),
        ]
        + [jax.ShapeDtypeStruct((n, ROWBLOCK, LANES), BF16) for n in (1, 2, 2, 2, 1)],
        in_specs=[smem] * 5 + [vmem, hbm, anywhere] + [hbm] * 7,
        out_specs=[vmem] * 6,
        scratch_shapes=[
            VMEM((8 * LINES, LANES), F32),
            VMEM((2 * HALF * M1, KP), BF16),
            VMEM((2 * HALF * M1, NP), F32),
            VMEM((STEP, NP), BF16),
            VMEM((STEP, NP), BF16),
            VMEM((N1 * 16, NP), F32),
            VMEM((BLOCK, LANES), F32),
            VMEM((ROWBLOCK, LANES), F32),
            VMEM((4, MG), BF16),
            VMEM((4, MG), BF16),
            VMEM((M2, NP), F32),
            VMEM((M3, NP), F32),
            VMEM((N1 * 16, HALF * M1), BF16),
            VMEM((N1 * 16, HALF * M1), BF16),
            VMEM((1, N1 * NP), F32),
            SMEM((16,), F32),
            SMEM((1024,), F32),
            pltpu.SemaphoreType.DMA((9,)),
        ],
        compiler_params=pltpu.CompilerParams(vmem_limit_bytes=26 << 20),
        interpret=interpret,
        name="density",
    )(place, mine, other, my_count, other_count, vals, stay(con_mine), con_other, stay(second), stay(third),
      stay(mix_hi), stay(mix_lo), stay(scale), stay(val_e), stay(con_e))


def pack_kernel(*refs):
    blocks, out, spread = refs[:5], refs[5], refs[6]
    stride = ROWBLOCK + 4
    for i in range(4):
        for m, block in enumerate((blocks[i + 1][0], blocks[i][1 if i else 0])):
            at = (2 * i + m) * stride
            spread[at : at + ROWBLOCK, :] = block.astype(F32)
    for ch in range(2 * WIDTH):
        for pp in range(HALF // 2):
            got = [spread[pl.ds(ch * HALF + 2 * pp + q, 8, stride=stride), :] for q in range(2)]
            out[pp * 16 : (pp + 1) * 16, ch * LANES : (ch + 1) * LANES] = jnp.concatenate(
                got, 0
            ).astype(BF16)


def pack_call(blocks, interpret=False):
    vmem = pl.BlockSpec(memory_space=VMEM)
    return pl.pallas_call(
        pack_kernel,
        out_shape=jax.ShapeDtypeStruct((8 * HALF, ROW), BF16),
        in_specs=[vmem] * 5,
        out_specs=vmem,
        scratch_shapes=[VMEM((8 * (ROWBLOCK + 4), LANES), F32)],
        compiler_params=pltpu.CompilerParams(vmem_limit_bytes=4 << 20),
        interpret=interpret,
        name="pack",
    )(*blocks)


def around(step):
    return jnp.where(step == 0, 0, jnp.where(step == 1, 3, jnp.where(step == 2, 1, 2)))


def assemble_kernel(place, *refs):
    cols = refs[:8]
    away_out, home_out, spread = refs[8:]
    me = place[0]
    band, y, x = me >> 7, (me >> 2) & 3, me & 3
    for v, col in enumerate(cols):
        for q in range(GCOL):
            at = v * COLROWS + q * BLOCK
            spread[at : at + BLOCK, :] = col[q].astype(F32)

    def assemble(j, carry):
        outer, inner = around(j >> 2), around(j & 3)
        dy = jnp.where(band == 0, outer, inner)
        dx = jnp.where(band == 0, inner, outer)
        base = (((y + dy) & 3) * 4 + ((x + dx) & 3)) * BLOCK
        weight = jnp.zeros((GROW, LANES), F32)
        for part in range(3):
            weight += spread[pl.ds(base + WIDTH * HALF + part, GROW, stride=COLROWS), :]
        other = pltpu.roll(weight, LANES - 16, 1)
        away = jnp.where(band == 0, other, weight)
        home = jnp.where(band == 0, weight, other)
        for pp in range(HALF // 2):
            ws = [
                [jnp.broadcast_to(w[:, 2 * pp + q : 2 * pp + q + 1], (GROW, LANES)) for q in range(2)]
                for w in (away, home)
            ]
            to = pl.ds(pl.multiple_of(j * GROW * HALF + pp * 16, 16), 16)
            for ch in range(WIDTH):
                got = [
                    spread[pl.ds(base + ch * HALF + 2 * pp + q, GROW, stride=COLROWS), :]
                    for q in range(2)
                ]
                where = slice(ch * LANES, (ch + 1) * LANES)
                for f, dest in enumerate((away_out, home_out)):
                    dest[to, where] = jnp.concatenate(
                        [got[0] * ws[f][0], got[1] * ws[f][1]], 0
                    ).astype(BF16)
        return carry

    lax.fori_loop(0, GCOL, assemble, 0)


def assemble_call(place, cols, interpret=False):
    vmem = pl.BlockSpec(memory_space=VMEM)
    return pl.pallas_call(
        assemble_kernel,
        out_shape=[jax.ShapeDtypeStruct((PANEL, NP), BF16)] * 2,
        in_specs=[pl.BlockSpec(memory_space=SMEM)] + [vmem] * 8,
        out_specs=[vmem] * 2,
        scratch_shapes=[VMEM((GROW * COLROWS, LANES), F32)],
        compiler_params=pltpu.CompilerParams(vmem_limit_bytes=14 << 20),
        interpret=interpret,
        name="assemble",
    )(place, *cols)


EARLY = 768
LATE = PANEL - EARLY
OVER = EARLY - 640


def flip_kernel(line, below, above, out):
    def turn(m, carry):
        where = pl.ds(pl.multiple_of(m * 256, 256), 256)
        out[where, :] = jnp.concatenate(
            [line[:, where], below[:, where], above[:OVER, where]], 0
        ).T
        return carry

    lax.fori_loop(0, ROW // 256, turn, 0)


def flip_call(line, below, above, interpret=False):
    vmem = pl.BlockSpec(memory_space=VMEM)
    return pl.pallas_call(
        flip_kernel,
        out_shape=jax.ShapeDtypeStruct((ROW, EARLY), BF16),
        in_specs=[vmem] * 3,
        out_specs=vmem,
        compiler_params=pltpu.CompilerParams(vmem_limit_bytes=8 << 20),
        interpret=interpret,
        name="flip",
    )(line, below, above)


def away_kernel(weighted, early, above, far_a, far_b, away_out, late_out, rows, sems):
    size = far_a.shape[0]
    copies = [
        pltpu.make_async_copy(above.at[pl.ds(OVER, 320 - OVER), :], rows.at[pl.ds(0, 320 - OVER), :], sems.at[0]),
        pltpu.make_async_copy(far_a, rows.at[pl.ds(320 - OVER, size), :], sems.at[1]),
        pltpu.make_async_copy(far_b, rows.at[pl.ds(320 - OVER + size, size), :], sems.at[2]),
    ]
    for copy in copies:
        copy.start()
    for copy in copies:
        copy.wait()

    def product(m, carry):
        where = pl.ds(pl.multiple_of(m * 256, 256), 256)
        part = rows[:, where].T
        late_out[where, :] = part
        away_out[where, :] = (
            jnp.dot(early[where, :], weighted[:EARLY, :], preferred_element_type=F32)
            + jnp.dot(part, weighted[EARLY:, :], preferred_element_type=F32)
        ).astype(BF16)
        return carry

    lax.fori_loop(0, ROW // 256, product, 0)


def away_call(weighted, early, above, far_a, far_b, interpret=False):
    vmem = pl.BlockSpec(memory_space=VMEM)
    anywhere = pl.BlockSpec(memory_space=pl.ANY)
    return pl.pallas_call(
        away_kernel,
        out_shape=(
            jax.ShapeDtypeStruct((ROW, NP), BF16),
            jax.ShapeDtypeStruct((ROW, LATE), BF16),
        ),
        in_specs=[vmem, vmem] + [anywhere] * 3,
        out_specs=(vmem, vmem),
        scratch_shapes=[VMEM((LATE, ROW), BF16), pltpu.SemaphoreType.DMA((3,))],
        compiler_params=pltpu.CompilerParams(vmem_limit_bytes=20 << 20),
        interpret=interpret,
        name="away",
    )(weighted, early, above, far_a, far_b)


def home_kernel(weighted, early, home_out):
    def product(m, carry):
        where = pl.ds(pl.multiple_of(m * 256, 256), 256)
        home_out[where, :] = jnp.dot(
            early[where, :], weighted[:EARLY, :], preferred_element_type=F32
        )
        return carry

    lax.fori_loop(0, ROW // 256, product, 0)


def home_call(weighted, early, interpret=False):
    vmem = pl.BlockSpec(memory_space=VMEM)
    return pl.pallas_call(
        home_kernel,
        out_shape=jax.ShapeDtypeStruct((ROW, NP), F32),
        in_specs=[vmem] * 2,
        out_specs=vmem,
        compiler_params=pltpu.CompilerParams(vmem_limit_bytes=16 << 20),
        interpret=interpret,
        name="home",
    )(weighted, early)


def finish_kernel(weighted, home, late, received, out, buffers, sems):
    copies = []
    for m in range(ROW // 256):
        where = slice(m * 256, (m + 1) * 256)
        slot = m % 2
        if m >= 2:
            copies[m - 2].wait()
        made = jnp.dot(late[where, :], weighted[EARLY:, :], preferred_element_type=F32)
        buffers[slot] = -(home[where, :] + made + received[where, :].astype(F32))
        copies.append(pltpu.make_async_copy(buffers.at[slot], out.at[0, pl.ds(m * 256, 256), :], sems.at[m]))
        copies[m].start()
    copies[-2].wait()
    copies[-1].wait()


def finish_call(weighted, home, late, received, interpret=False):
    vmem = pl.BlockSpec(memory_space=VMEM)
    return pl.pallas_call(
        finish_kernel,
        out_shape=jax.ShapeDtypeStruct((1, ROW, NP), F32),
        in_specs=[vmem] * 4,
        out_specs=pl.BlockSpec(memory_space=pltpu.HBM),
        scratch_shapes=[VMEM((2, 256, NP), F32), pltpu.SemaphoreType.DMA((ROW // 256,))],
        compiler_params=pltpu.CompilerParams(vmem_limit_bytes=16 << 20),
        interpret=interpret,
        name="finish",
    )(weighted, home, late, received)


PLANE = ("band", "gcol_0", "gcol_1")


def turned(array, phase, step):
    pairs = []
    for band in range(2):
        along_x = (band == 0) == (phase == 0)
        for y in range(4):
            for x in range(4):
                to = (y, (x + step) % 4) if along_x else ((y + step) % 4, x)
                pairs.append((band * 16 + y * 4 + x, band * 16 + to[0] * 4 + to[1]))
    return lax.ppermute(array, PLANE, pairs)


def along(array, step):
    pairs = []
    for band in range(2):
        for z in range(GROW):
            to = (z + step) % GROW if band == 0 else (z - step) % GROW
            pairs.append((band * GROW + z, band * GROW + to))
    return lax.ppermute(array, ("band", "grow"), pairs)


def swap(array):
    return lax.ppermute(array, "band", [(0, 1), (1, 0)])


def per_device(
    valence_orbitals,
    conduction_orbitals,
    valence_energy,
    conduction_energy,
    coulomb_root,
    pair_bands,
    slot_counts,
):
    place = lax.axis_index(("band", "grow", "gcol_0", "gcol_1")).astype(jnp.int32).reshape(1)
    other_con = swap(conduction_orbitals)
    other_pairs, other_count = swap(pair_bands), swap(slot_counts)
    vals = ready_call(valence_orbitals)
    col, *rows = density_call(
        place, pair_bands, other_pairs, slot_counts, other_count, valence_energy, conduction_energy,
        vals, conduction_orbitals, other_con, coulomb_root.reshape(1, N1 * NP),
    )
    return exchange(place, col, rows)


def exchange(place, col, rows):
    rows = [rows[0]] + [along(rows[i], i) for i in range(1, 5)]
    col = lax.all_to_all(col, ("gcol_0", "gcol_1"), 0, 0, tiled=True)
    row = pack_call(rows)
    main, other = [col], [swap(col)]
    for _ in range(1, 5):
        main.append(along(main[-1], 1))
    for _ in range(1, 4):
        other.append(along(other[-1], 1))
    rings = []
    for i in range(4):
        rings += [main[i + 1], other[i]]
    far = turned(row, 0, 2)
    below, above = turned(row, 0, 1), turned(row, 0, -1)
    line = jnp.concatenate([row, below, above, far], 0)
    half = line.shape[0] // 2
    below, above = turned(line, 1, 1), turned(line, 1, -1)
    far_a, far_b = turned(below[:half], 1, 1), turned(above[half:], 1, -1)
    weighted_away, weighted_home = assemble_call(place, rings)
    early = flip_call(line, below, above)
    away, late = away_call(weighted_away, early, above, far_a, far_b)
    received = swap(away)
    home = home_call(weighted_home, early)
    return finish_call(weighted_home, home, late, received)


def solution(mesh):
    finer = Mesh(
        mesh.devices.reshape(mesh.shape["band"], mesh.shape["grow"], 4, 4),
        ("band", "grow", "gcol_0", "gcol_1"),
    )
    everywhere = ("band", "grow", "gcol_0", "gcol_1")
    in_specs = (P(), P(everywhere, None), P(), P(), P(), P(None, everywhere), P(everywhere))
    return jax.shard_map(
        per_device,
        mesh=finer,
        in_specs=in_specs,
        out_specs=P("band", "grow", ("gcol_0", "gcol_1")),
        check_vma=False,
    )
```

profile of v0, /device:TPU:1, one launch (start us, length us, event | category | flops | bytes accessed | tf_op | source)
XLA Modules:
  0.0 119.9 jit_solution(12888136892374336506)
XLA Ops:
  0.0 3.2 %collective-permute-start.2 = (bf16[4,98304]{1,0:T(4,128)(2,1)}, bf16[4,98304]{1,0:T(4,128)(2,1)S(1)}, u32[]{:S(2)}, u32[]{:S(2)}) collective-permute-start(bf16[4,98304]{1,0:T(4,128)(2,1)} %refs_0_.1), channel_id=1, source_target_pairs={{0,128},{128,0},{1,129},{129,1},{2,130},{130,2},{3,131},{131,3},{4... | collective-permute-start | bytes 2359304 | tf_op jit(solution)/shard_map/ppermute | solution.py:517
  3.2 0.0 collective-permute-start.1
  3.2 0.5 collective-permute-start
  4.4 0.0 copy-start.2
  4.4 2.1 %ready.1.vals = f32[12352,128]{1,0:T(8,128)S(1)} custom-call(bf16[16,98304]{1,0:T(8,128)(2,1)} %source.1), custom_call_target="tpu_custom_call" | custom-call | tf_op jit(solution)/shard_map/ready/pallas_call | solution.py:83
  6.5 0.0 copy-start
  6.5 2.6 %copy-done = f32[12352,128]{1,0:T(8,128)} copy-done((f32[12352,128]{1,0:T(8,128)}, f32[12352,128]{1,0:T(8,128)S(1)}, u32[]{:S(2)}) %copy-start) | copy-done | bytes 6324248
  9.2 0.0 collective-permute-done.1.other_count
  9.2 0.0 collective-permute-done.other
  9.2 0.0 collective-permute-done.2.refs_1_
  9.2 0.0 copy-done.2
  9.2 0.0 copy-start.1
  9.2 2.8 %copy-done.1 = f32[12352,128]{1,0:T(8,128)S(1)} copy-done((f32[12352,128]{1,0:T(8,128)S(1)}, f32[12352,128]{1,0:T(8,128)}, u32[]{:S(2)}) %copy-start.1) | copy-done | bytes 6324248
  12.0 12.0 %density.1 = (bf16[16,64,128]{2,1,0:T(8,128)(2,1)S(1)}, bf16[1,120,128]{2,1,0:T(8,128)(2,1)S(1)}, bf16[2,120,128]{2,1,0:T(8,128)(2,1)S(1)}, bf16[2,120,128]{2,1,...) custom-call(s32[1]{0:T(128)} %bitcast.place, s32[2,20]{1,0:T(2,128)S(1)} %copy-done.2, ...), custom_call_target="tpu_custom_call" | custom-call | tf_op jit(solution)/shard_map/density/pallas_call | solution.py:244
  24.0 3.9 %collective-permute-start.11 = (bf16[2,120,128]{2,1,0:T(8,128)(2,1)S(1)}, bf16[2,120,128]{2,1,0:T(8,128)(2,1)S(1)}, u32[]{:S(2)}, u32[]{:S(2)}) collective-permute-start(bf16[2,120,128]{2,1,0:T(8,128)(2,1)S(1)} %get-tuple-element.18), channel_id=1, source_target_pairs={{0,16},{16,32},{32,48},{48,64},{64,80},{80,96},{96,112},{112,0},{1... | collective-permute-start | bytes 184328 | tf_op jit(solution)/shard_map/ppermute | solution.py:513
  28.0 1.1 collective-permute-start.12
  29.1 0.5 collective-permute-start.13
  29.6 4.4 %collective-permute-start.14 = (bf16[1,120,128]{2,1,0:T(8,128)(2,1)S(1)}, bf16[1,120,128]{2,1,0:T(8,128)(2,1)S(1)}, u32[]{:S(2)}, u32[]{:S(2)}) collective-permute-start(bf16[1,120,128]{2,1,0:T(8,128)(2,1)S(1)} %get-tuple-element.21), channel_id=1, source_target_pairs={{0,64},{16,80},{32,96},{48,112},{64,0},{80,16},{96,32},{112,48},{1... | collective-permute-start | bytes 92168 | tf_op jit(solution)/shard_map/ppermute | solution.py:513
  34.0 3.5 %collective-permute-done.14.refs_4_ = bf16[1,120,128]{2,1,0:T(8,128)(2,1)S(1)} collective-permute-done((bf16[1,120,128]{2,1,0:T(8,128)(2,1)S(1)}, bf16[1,120,128]{2,1,0:T(8,128)(2,1)S(1)}, u32[]{:S(2)}, u32[]{:S(2)}) %collective-permute-start.14) | collective-permute-done | bytes 30752 | tf_op jit(solution)/shard_map/ppermute | solution.py:513
  37.6 0.0 collective-permute-done.11.refs_1_
  37.6 0.0 collective-permute-done.12.refs_2_
  37.6 0.0 collective-permute-done.13.refs_3_
  37.6 0.1 pack.1
  37.7 3.0 %collective-permute-start.17 = (bf16[80,1536]{1,0:T(8,128)(2,1)S(1)}, bf16[80,1536]{1,0:T(8,128)(2,1)S(1)}, u32[]{:S(2)}, u32[]{:S(2)}) collective-permute-start(bf16[80,1536]{1,0:T(8,128)(2,1)S(1)} %pack.1), channel_id=1, source_target_pairs={{0,2},{1,3},{2,0},{3,1},{4,6},{5,7},{6,4},{7,5},{8,10},{9,11},{10,... | collective-permute-start | bytes 737288 | tf_op jit(solution)/shard_map/ppermute | solution.py:504
  40.7 0.8 collective-permute-start.16
  41.5 0.7 collective-permute-start.15
  42.1 2.4 %collective-permute-done.17 = bf16[80,1536]{1,0:T(8,128)(2,1)S(1)} collective-permute-done((bf16[80,1536]{1,0:T(8,128)(2,1)S(1)}, bf16[80,1536]{1,0:T(8,128)(2,1)S(1)}, u32[]{:S(2)}, u32[]{:S(2)}) %collective-permute-start.17) | collective-permute-done | bytes 245792 | tf_op jit(solution)/shard_map/ppermute | solution.py:504
  44.6 3.1 %collective-permute-done.16 = bf16[80,1536]{1,0:T(8,128)(2,1)S(1)} collective-permute-done((bf16[80,1536]{1,0:T(8,128)(2,1)S(1)}, bf16[80,1536]{1,0:T(8,128)(2,1)S(1)}, u32[]{:S(2)}, u32[]{:S(2)}) %collective-permute-start.16) | collective-permute-done | bytes 245792 | tf_op jit(solution)/shard_map/ppermute | solution.py:504
  47.7 0.1 collective-permute-done.15
  47.7 0.1 pad_maximum_fusion.line
  47.8 2.8 %collective-permute-start.19 = (bf16[320,1536]{1,0:T(8,128)(2,1)S(1)}, bf16[320,1536]{1,0:T(8,128)(2,1)S(1)}, u32[]{:S(2)}, u32[]{:S(2)}) collective-permute-start(bf16[320,1536]{1,0:T(8,128)(2,1)S(1)} %pad_maximum_fusion.line), channel_id=1, source_target_pairs={{0,12},{1,13},{2,14},{3,15},{4,0},{5,1},{6,2},{7,3},{8,4},{9,5},{1... | collective-permute-start | bytes 2949128 | tf_op jit(solution)/shard_map/ppermute | solution.py:504
  50.6 0.0 collective-permute-start.18
  50.6 18.5 %all_to_all.5 = bf16[16,64,128]{2,1,0:T(8,128)(2,1)S(1)} all-to-all(bf16[16,64,128]{2,1,0:T(8,128)(2,1)S(1)} %get-tuple-element.15), channel_id=1, replica_groups=mesh['band'=2,'grow'=8,'gcol_0'=4,'gcol_1'=4] {'gcol_0','gcol_1'}, dimensions={0} | all-to-all | bytes 524288 | tf_op jit(solution)/shard_map/all_to_all | solution.py:542
  69.1 3.4 %collective-permute-start.4 = (bf16[16,64,128]{2,1,0:T(8,128)(2,1)S(1)}, bf16[16,64,128]{2,1,0:T(8,128)(2,1)S(1)}, u32[]{:S(2)}, u32[]{:S(2)}) collective-permute-start(bf16[16,64,128]{2,1,0:T(8,128)(2,1)S(1)} %all_to_all.5), channel_id=1, source_target_pairs={{0,128},{128,0},{1,129},{129,1},{2,130},{130,2},{3,131},{131,3},{4... | collective-permute-start | bytes 786440 | tf_op jit(solution)/shard_map/ppermute | solution.py:517
  72.4 2.6 %collective-permute-start.3 = (bf16[16,64,128]{2,1,0:T(8,128)(2,1)S(1)}, bf16[16,64,128]{2,1,0:T(8,128)(2,1)S(1)}, u32[]{:S(2)}, u32[]{:S(2)}) collective-permute-start(bf16[16,64,128]{2,1,0:T(8,128)(2,1)S(1)} %all_to_all.5), channel_id=1, source_target_pairs={{0,16},{16,32},{32,48},{48,64},{64,80},{80,96},{96,112},{112,0},{1... | collective-permute-start | bytes 786440 | tf_op jit(solution)/shard_map/ppermute | solution.py:513
  75.1 0.0 collective-permute-done.4.refs_1_
  75.1 1.2 collective-permute-start.6
  76.2 2.2 %collective-permute-done.3.refs_0_ = bf16[16,64,128]{2,1,0:T(8,128)(2,1)S(1)} collective-permute-done((bf16[16,64,128]{2,1,0:T(8,128)(2,1)S(1)}, bf16[16,64,128]{2,1,0:T(8,128)(2,1)S(1)}, u32[]{:S(2)}, u32[]{:S(2)}) %collective-permute-start.3) | collective-permute-done | bytes 262176 | tf_op jit(solution)/shard_map/ppermute | solution.py:513
  78.4 3.1 %collective-permute-start.5 = (bf16[16,64,128]{2,1,0:T(8,128)(2,1)S(1)}, bf16[16,64,128]{2,1,0:T(8,128)(2,1)S(1)}, u32[]{:S(2)}, u32[]{:S(2)}) collective-permute-start(bf16[16,64,128]{2,1,0:T(8,128)(2,1)S(1)} %collective-permute-done.3.refs_0_), channel_id=1, source_target_pairs={{0,16},{16,32},{32,48},{48,64},{64,80},{80,96},{96,112},{112,0},{1... | collective-permute-start | bytes 786440 | tf_op jit(solution)/shard_map/ppermute | solution.py:513
  81.5 0.0 collective-permute-done.6.refs_3_
  81.5 2.8 %collective-permute-start.8 = (bf16[16,64,128]{2,1,0:T(8,128)(2,1)S(1)}, bf16[16,64,128]{2,1,0:T(8,128)(2,1)S(1)}, u32[]{:S(2)}, u32[]{:S(2)}) collective-permute-start(bf16[16,64,128]{2,1,0:T(8,128)(2,1)S(1)} %collective-permute-done.6.refs_3_), channel_id=1, source_target_pairs={{0,16},{16,32},{32,48},{48,64},{64,80},{80,96},{96,112},{112,0},{1... | collective-permute-start | bytes 786440 | tf_op jit(solution)/shard_map/ppermute | solution.py:513
  84.3 0.5 collective-permute-done.5.refs_2_
  84.8 3.1 %collective-permute-start.7 = (bf16[16,64,128]{2,1,0:T(8,128)(2,1)S(1)}, bf16[16,64,128]{2,1,0:T(8,128)(2,1)S(1)}, u32[]{:S(2)}, u32[]{:S(2)}) collective-permute-start(bf16[16,64,128]{2,1,0:T(8,128)(2,1)S(1)} %collective-permute-done.5.refs_2_), channel_id=1, source_target_pairs={{0,16},{16,32},{32,48},{48,64},{64,80},{80,96},{96,112},{112,0},{1... | collective-permute-start | bytes 786440 | tf_op jit(solution)/shard_map/ppermute | solution.py:513
  87.9 0.0 collective-permute-done.19.above
  88.0 1.3 %collective-permute-start.21 = (bf16[160,1536]{1,0:T(8,128)(2,1)S(1)}, bf16[160,1536]{1,0:T(8,128)(2,1)S(1)}, u32[]{:S(2)}, u32[]{:S(2)}) collective-permute-start(bf16[160,1536]{1,0:T(8,128)(2,1)S(1)} %slice.9), channel_id=1, source_target_pairs={{0,12},{1,13},{2,14},{3,15},{4,0},{5,1},{6,2},{7,3},{8,4},{9,5},{1... | collective-permute-start | bytes 1474568 | tf_op jit(solution)/shard_map/ppermute | solution.py:504
  89.3 0.0 collective-permute-done.18.below
  89.3 0.3 collective-permute-start.20
  89.7 0.0 collective-permute-done.8.refs_5_
  89.7 1.1 collective-permute-start.10
  90.8 0.5 collective-permute-done.7.refs_4_
  91.3 3.1 %collective-permute-start.9 = (bf16[16,64,128]{2,1,0:T(8,128)(2,1)S(1)}, bf16[16,64,128]{2,1,0:T(8,128)(2,1)S(1)}, u32[]{:S(2)}, u32[]{:S(2)}) collective-permute-start(bf16[16,64,128]{2,1,0:T(8,128)(2,1)S(1)} %collective-permute-done.7.refs_4_), channel_id=1, source_target_pairs={{0,16},{16,32},{32,48},{48,64},{64,80},{80,96},{96,112},{112,0},{1... | collective-permute-start | bytes 786440 | tf_op jit(solution)/shard_map/ppermute | solution.py:513
  94.4 0.9 flip.1.early
  95.3 0.0 collective-permute-done.10.refs_7_
  95.3 2.4 %collective-permute-done.9.refs_6_ = bf16[16,64,128]{2,1,0:T(8,128)(2,1)S(1)} collective-permute-done((bf16[16,64,128]{2,1,0:T(8,128)(2,1)S(1)}, bf16[16,64,128]{2,1,0:T(8,128)(2,1)S(1)}, u32[]{:S(2)}, u32[]{:S(2)}) %collective-permute-start.9) | collective-permute-done | bytes 262176 | tf_op jit(solution)/shard_map/ppermute | solution.py:513
  97.7 3.2 %assemble.1 = (bf16[1280,768]{1,0:T(8,128)(2,1)S(1)}, bf16[1280,768]{1,0:T(8,128)(2,1)S(1)}) custom-call(s32[1]{0:T(128)} %bitcast.place, bf16[16,64,128]{2,1,0:T(8,128)(2,1)S(1)} %collective-permute-done.3.refs_0_, bf16[16,64,128]{2,1,0:T(8,128)(2,1)S(1)} %collective-permute-done.4.refs_1_, bf16[16,64,128]{2,1,0:T(8,128)(2,1)S(1)} %collective-permute-done.5.refs_2_, ...), custom_call_target="tpu_custom_call" | custom-call | tf_op jit(solution)/shard_map/assemble/pallas_call | solution.py:356
  100.9 0.0 collective-permute-done.21.far_b
  100.9 0.0 collective-permute-done.20.far_a
  100.9 5.0 %away.1 = (bf16[1536,768]{1,0:T(8,128)(2,1)S(1)}, bf16[1536,512]{1,0:T(8,128)(2,1)S(1)}) custom-call(bf16[1280,768]{1,0:T(8,128)(2,1)S(1)} %get-tuple-element.22.weighted, bf16[1536,768]{1,0:T(8,128)(2,1)S(1)} %flip.1.early, bf16[320,1536]{1,0:T(8,128)(2,1)S(1)} %collective-permute-done.19.above, bf16[160,1536]{1,0:T(8,128)(2,1)S(1)} %collective-permute-done.20.far_a, ...), custom_call_target="tpu_custom_call" | custom-call | tf_op jit(solution)/shard_map/away/pallas_call | solution.py:425
  106.0 5.2 %collective-permute-start.22 = (bf16[1536,768]{1,0:T(8,128)(2,1)S(1)}, bf16[1536,768]{1,0:T(8,128)(2,1)S(1)}, u32[]{:S(2)}, u32[]{:S(2)}) collective-permute-start(bf16[1536,768]{1,0:T(8,128)(2,1)S(1)} %get-tuple-element.24), channel_id=1, source_target_pairs={{0,128},{128,0},{1,129},{129,1},{2,130},{130,2},{3,131},{131,3},{4... | collective-permute-start | bytes 7077896 | tf_op jit(solution)/shard_map/ppermute | solution.py:517
  111.1 2.9 %home.1 = f32[1536,768]{1,0:T(8,128)S(1)} custom-call(bf16[1280,768]{1,0:T(8,128)(2,1)S(1)} %get-tuple-element.16.weighted, bf16[1536,768]{1,0:T(8,128)(2,1)S(1)} %flip.1.early), custom_call_target="tpu_custom_call" | custom-call | tf_op jit(solution)/shard_map/home/pallas_call | solution.py:453
  114.0 1.3 %collective-permute-done.22.received = bf16[1536,768]{1,0:T(8,128)(2,1)S(1)} collective-permute-done((bf16[1536,768]{1,0:T(8,128)(2,1)S(1)}, bf16[1536,768]{1,0:T(8,128)(2,1)S(1)}, u32[]{:S(2)}, u32[]{:S(2)}) %collective-permute-start.22) | collective-permute-done | bytes 2359328 | tf_op jit(solution)/shard_map/ppermute | solution.py:517
  115.3 4.5 %finish.1 = f32[1,1536,768]{2,1,0:T(8,128)} custom-call(bf16[1280,768]{1,0:T(8,128)(2,1)S(1)} %get-tuple-element.16.weighted, f32[1536,768]{1,0:T(8,128)S(1)} %home.1, bf16[1536,512]{1,0:T(8,128)(2,1)S(1)} %get-tuple-element.23.late, bf16[1536,768]{1,0:T(8,128)(2,1)S(1)} %collective-permute-done.22.received), custom_call_target="tpu_custom_call" | custom-call | tf_op jit(solution)/shard_map/finish/pallas_call | solution.py:481
  (2 shorter events, 0.1 us)
Async XLA Ops:
  0.0 9.2 %collective-permute-start.2 = (bf16[4,98304]{1,0:T(4,128)(2,1)}, bf16[4,98304]{1,0:T(4,128)(2,1)S(1)}, u32[]{:S(2)}, u32[]{:S(2)}) collective-permute-start(bf16[4,98304]{1,0:T(4,128)(2,1)} %refs_0_.1), channel_id=1, source_target_pairs={{0,128},{128,0},{1,129},{129,1},{2,130},{130,2},{3,131},{131,3},{4... | collective-permute-start | bytes 2359304 | tf_op jit(solution)/shard_map/ppermute | solution.py:517
  3.2 6.0 %collective-permute-start.1 = (s32[1]{0:T(128)}, s32[1]{0:T(128)}, u32[]{:S(2)}, u32[]{:S(2)}) collective-permute-start(s32[1]{0:T(128)} %param.17), channel_id=1, source_target_pairs={{0,128},{128,0},{1,129},{129,1},{2,130},{130,2},{3,131},{131,3},{4... | collective-permute-start | bytes 20 | tf_op jit(solution)/shard_map/ppermute | solution.py:517
  3.2 6.0 %collective-permute-start = (s32[2,20]{1,0:T(2,128)}, s32[2,20]{1,0:T(2,128)S(1)}, u32[]{:S(2)}, u32[]{:S(2)}) collective-permute-start(s32[2,20]{1,0:T(2,128)} %mine.1), channel_id=1, source_target_pairs={{0,128},{128,0},{1,129},{129,1},{2,130},{130,2},{3,131},{131,3},{4... | collective-permute-start | bytes 488 | tf_op jit(solution)/shard_map/ppermute | solution.py:517
  4.4 4.8 %copy-start.2 = (s32[2,20]{1,0:T(2,128)S(1)}, s32[2,20]{1,0:T(2,128)}, u32[]{:S(2)}) copy-start(s32[2,20]{1,0:T(2,128)} %mine.1) | copy-start | bytes 484
  6.5 2.6 %copy-start = (f32[12352,128]{1,0:T(8,128)}, f32[12352,128]{1,0:T(8,128)S(1)}, u32[]{:S(2)}) copy-start(f32[12352,128]{1,0:T(8,128)S(1)} %ready.1.vals) | copy-start | bytes 18972676
  9.2 2.8 %copy-start.1 = (f32[12352,128]{1,0:T(8,128)S(1)}, f32[12352,128]{1,0:T(8,128)}, u32[]{:S(2)}) copy-start(f32[12352,128]{1,0:T(8,128)} %copy-done) | copy-start | bytes 18972676
  24.0 13.5 %collective-permute-start.11 = (bf16[2,120,128]{2,1,0:T(8,128)(2,1)S(1)}, bf16[2,120,128]{2,1,0:T(8,128)(2,1)S(1)}, u32[]{:S(2)}, u32[]{:S(2)}) collective-permute-start(bf16[2,120,128]{2,1,0:T(8,128)(2,1)S(1)} %get-tuple-element.18), channel_id=1, source_target_pairs={{0,16},{16,32},{32,48},{48,64},{64,80},{80,96},{96,112},{112,0},{1... | collective-permute-start | bytes 184328 | tf_op jit(solution)/shard_map/ppermute | solution.py:513
  28.0 9.6 %collective-permute-start.12 = (bf16[2,120,128]{2,1,0:T(8,128)(2,1)S(1)}, bf16[2,120,128]{2,1,0:T(8,128)(2,1)S(1)}, u32[]{:S(2)}, u32[]{:S(2)}) collective-permute-start(bf16[2,120,128]{2,1,0:T(8,128)(2,1)S(1)} %get-tuple-element.19), channel_id=1, source_target_pairs={{0,32},{16,48},{32,64},{48,80},{64,96},{80,112},{96,0},{112,16},{1... | collective-permute-start | bytes 184328 | tf_op jit(solution)/shard_map/ppermute | solution.py:513
  29.1 8.5 %collective-permute-start.13 = (bf16[2,120,128]{2,1,0:T(8,128)(2,1)S(1)}, bf16[2,120,128]{2,1,0:T(8,128)(2,1)S(1)}, u32[]{:S(2)}, u32[]{:S(2)}) collective-permute-start(bf16[2,120,128]{2,1,0:T(8,128)(2,1)S(1)} %get-tuple-element.20), channel_id=1, source_target_pairs={{0,48},{16,64},{32,80},{48,96},{64,112},{80,0},{96,16},{112,32},{1... | collective-permute-start | bytes 184328 | tf_op jit(solution)/shard_map/ppermute | solution.py:513
  29.6 8.0 %collective-permute-start.14 = (bf16[1,120,128]{2,1,0:T(8,128)(2,1)S(1)}, bf16[1,120,128]{2,1,0:T(8,128)(2,1)S(1)}, u32[]{:S(2)}, u32[]{:S(2)}) collective-permute-start(bf16[1,120,128]{2,1,0:T(8,128)(2,1)S(1)} %get-tuple-element.21), channel_id=1, source_target_pairs={{0,64},{16,80},{32,96},{48,112},{64,0},{80,16},{96,32},{112,48},{1... | collective-permute-start | bytes 92168 | tf_op jit(solution)/shard_map/ppermute | solution.py:513
  37.7 6.9 %collective-permute-start.17 = (bf16[80,1536]{1,0:T(8,128)(2,1)S(1)}, bf16[80,1536]{1,0:T(8,128)(2,1)S(1)}, u32[]{:S(2)}, u32[]{:S(2)}) collective-permute-start(bf16[80,1536]{1,0:T(8,128)(2,1)S(1)} %pack.1), channel_id=1, source_target_pairs={{0,2},{1,3},{2,0},{3,1},{4,6},{5,7},{6,4},{7,5},{8,10},{9,11},{10,... | collective-permute-start | bytes 737288 | tf_op jit(solution)/shard_map/ppermute | solution.py:504
  40.7 7.0 %collective-permute-start.16 = (bf16[80,1536]{1,0:T(8,128)(2,1)S(1)}, bf16[80,1536]{1,0:T(8,128)(2,1)S(1)}, u32[]{:S(2)}, u32[]{:S(2)}) collective-permute-start(bf16[80,1536]{1,0:T(8,128)(2,1)S(1)} %pack.1), channel_id=1, source_target_pairs={{0,3},{1,0},{2,1},{3,2},{4,7},{5,4},{6,5},{7,6},{8,11},{9,8},{10,9... | collective-permute-start | bytes 737288 | tf_op jit(solution)/shard_map/ppermute | solution.py:504
  41.5 6.3 %collective-permute-start.15 = (bf16[80,1536]{1,0:T(8,128)(2,1)S(1)}, bf16[80,1536]{1,0:T(8,128)(2,1)S(1)}, u32[]{:S(2)}, u32[]{:S(2)}) collective-permute-start(bf16[80,1536]{1,0:T(8,128)(2,1)S(1)} %pack.1), channel_id=1, source_target_pairs={{0,1},{1,2},{2,3},{3,0},{4,5},{5,6},{6,7},{7,4},{8,9},{9,10},{10,1... | collective-permute-start | bytes 737288 | tf_op jit(solution)/shard_map/ppermute | solution.py:504
  47.8 40.2 %collective-permute-start.19 = (bf16[320,1536]{1,0:T(8,128)(2,1)S(1)}, bf16[320,1536]{1,0:T(8,128)(2,1)S(1)}, u32[]{:S(2)}, u32[]{:S(2)}) collective-permute-start(bf16[320,1536]{1,0:T(8,128)(2,1)S(1)} %pad_maximum_fusion.line), channel_id=1, source_target_pairs={{0,12},{1,13},{2,14},{3,15},{4,0},{5,1},{6,2},{7,3},{8,4},{9,5},{1... | collective-permute-start | bytes 2949128 | tf_op jit(solution)/shard_map/ppermute | solution.py:504
  50.6 38.7 %collective-permute-start.18 = (bf16[320,1536]{1,0:T(8,128)(2,1)S(1)}, bf16[320,1536]{1,0:T(8,128)(2,1)S(1)}, u32[]{:S(2)}, u32[]{:S(2)}) collective-permute-start(bf16[320,1536]{1,0:T(8,128)(2,1)S(1)} %pad_maximum_fusion.line), channel_id=1, source_target_pairs={{0,4},{1,5},{2,6},{3,7},{4,8},{5,9},{6,10},{7,11},{8,12},{9,13},{1... | collective-permute-start | bytes 2949128 | tf_op jit(solution)/shard_map/ppermute | solution.py:504
  69.1 6.0 %collective-permute-start.4 = (bf16[16,64,128]{2,1,0:T(8,128)(2,1)S(1)}, bf16[16,64,128]{2,1,0:T(8,128)(2,1)S(1)}, u32[]{:S(2)}, u32[]{:S(2)}) collective-permute-start(bf16[16,64,128]{2,1,0:T(8,128)(2,1)S(1)} %all_to_all.5), channel_id=1, source_target_pairs={{0,128},{128,0},{1,129},{129,1},{2,130},{130,2},{3,131},{131,3},{4... | collective-permute-start | bytes 786440 | tf_op jit(solution)/shard_map/ppermute | solution.py:517
  72.4 6.0 %collective-permute-start.3 = (bf16[16,64,128]{2,1,0:T(8,128)(2,1)S(1)}, bf16[16,64,128]{2,1,0:T(8,128)(2,1)S(1)}, u32[]{:S(2)}, u32[]{:S(2)}) collective-permute-start(bf16[16,64,128]{2,1,0:T(8,128)(2,1)S(1)} %all_to_all.5), channel_id=1, source_target_pairs={{0,16},{16,32},{32,48},{48,64},{64,80},{80,96},{96,112},{112,0},{1... | collective-permute-start | bytes 786440 | tf_op jit(solution)/shard_map/ppermute | solution.py:513
  75.1 6.4 %collective-permute-start.6 = (bf16[16,64,128]{2,1,0:T(8,128)(2,1)S(1)}, bf16[16,64,128]{2,1,0:T(8,128)(2,1)S(1)}, u32[]{:S(2)}, u32[]{:S(2)}) collective-permute-start(bf16[16,64,128]{2,1,0:T(8,128)(2,1)S(1)} %collective-permute-done.4.refs_1_), channel_id=1, source_target_pairs={{0,16},{16,32},{32,48},{48,64},{64,80},{80,96},{96,112},{112,0},{1... | collective-permute-start | bytes 786440 | tf_op jit(solution)/shard_map/ppermute | solution.py:513
  78.4 6.4 %collective-permute-start.5 = (bf16[16,64,128]{2,1,0:T(8,128)(2,1)S(1)}, bf16[16,64,128]{2,1,0:T(8,128)(2,1)S(1)}, u32[]{:S(2)}, u32[]{:S(2)}) collective-permute-start(bf16[16,64,128]{2,1,0:T(8,128)(2,1)S(1)} %collective-permute-done.3.refs_0_), channel_id=1, source_target_pairs={{0,16},{16,32},{32,48},{48,64},{64,80},{80,96},{96,112},{112,0},{1... | collective-permute-start | bytes 786440 | tf_op jit(solution)/shard_map/ppermute | solution.py:513
  81.5 8.1 %collective-permute-start.8 = (bf16[16,64,128]{2,1,0:T(8,128)(2,1)S(1)}, bf16[16,64,128]{2,1,0:T(8,128)(2,1)S(1)}, u32[]{:S(2)}, u32[]{:S(2)}) collective-permute-start(bf16[16,64,128]{2,1,0:T(8,128)(2,1)S(1)} %collective-permute-done.6.refs_3_), channel_id=1, source_target_pairs={{0,16},{16,32},{32,48},{48,64},{64,80},{80,96},{96,112},{112,0},{1... | collective-permute-start | bytes 786440 | tf_op jit(solution)/shard_map/ppermute | solution.py:513
  84.8 6.4 %collective-permute-start.7 = (bf16[16,64,128]{2,1,0:T(8,128)(2,1)S(1)}, bf16[16,64,128]{2,1,0:T(8,128)(2,1)S(1)}, u32[]{:S(2)}, u32[]{:S(2)}) collective-permute-start(bf16[16,64,128]{2,1,0:T(8,128)(2,1)S(1)} %collective-permute-done.5.refs_2_), channel_id=1, source_target_pairs={{0,16},{16,32},{32,48},{48,64},{64,80},{80,96},{96,112},{112,0},{1... | collective-permute-start | bytes 786440 | tf_op jit(solution)/shard_map/ppermute | solution.py:513
  88.0 12.9 %collective-permute-start.21 = (bf16[160,1536]{1,0:T(8,128)(2,1)S(1)}, bf16[160,1536]{1,0:T(8,128)(2,1)S(1)}, u32[]{:S(2)}, u32[]{:S(2)}) collective-permute-start(bf16[160,1536]{1,0:T(8,128)(2,1)S(1)} %slice.9), channel_id=1, source_target_pairs={{0,12},{1,13},{2,14},{3,15},{4,0},{5,1},{6,2},{7,3},{8,4},{9,5},{1... | collective-permute-start | bytes 1474568 | tf_op jit(solution)/shard_map/ppermute | solution.py:504
  89.3 11.6 %collective-permute-start.20 = (bf16[160,1536]{1,0:T(8,128)(2,1)S(1)}, bf16[160,1536]{1,0:T(8,128)(2,1)S(1)}, u32[]{:S(2)}, u32[]{:S(2)}) collective-permute-start(bf16[160,1536]{1,0:T(8,128)(2,1)S(1)} %slice.8), channel_id=1, source_target_pairs={{0,4},{1,5},{2,6},{3,7},{4,8},{5,9},{6,10},{7,11},{8,12},{9,13},{1... | collective-permute-start | bytes 1474568 | tf_op jit(solution)/shard_map/ppermute | solution.py:504
  89.7 5.7 %collective-permute-start.10 = (bf16[16,64,128]{2,1,0:T(8,128)(2,1)S(1)}, bf16[16,64,128]{2,1,0:T(8,128)(2,1)S(1)}, u32[]{:S(2)}, u32[]{:S(2)}) collective-permute-start(bf16[16,64,128]{2,1,0:T(8,128)(2,1)S(1)} %collective-permute-done.8.refs_5_), channel_id=1, source_target_pairs={{0,16},{16,32},{32,48},{48,64},{64,80},{80,96},{96,112},{112,0},{1... | collective-permute-start | bytes 786440 | tf_op jit(solution)/shard_map/ppermute | solution.py:513
  91.3 6.4 %collective-permute-start.9 = (bf16[16,64,128]{2,1,0:T(8,128)(2,1)S(1)}, bf16[16,64,128]{2,1,0:T(8,128)(2,1)S(1)}, u32[]{:S(2)}, u32[]{:S(2)}) collective-permute-start(bf16[16,64,128]{2,1,0:T(8,128)(2,1)S(1)} %collective-permute-done.7.refs_4_), channel_id=1, source_target_pairs={{0,16},{16,32},{32,48},{48,64},{64,80},{80,96},{96,112},{112,0},{1... | collective-permute-start | bytes 786440 | tf_op jit(solution)/shard_map/ppermute | solution.py:513
  106.0 9.3 %collective-permute-start.22 = (bf16[1536,768]{1,0:T(8,128)(2,1)S(1)}, bf16[1536,768]{1,0:T(8,128)(2,1)S(1)}, u32[]{:S(2)}, u32[]{:S(2)}) collective-permute-start(bf16[1536,768]{1,0:T(8,128)(2,1)S(1)} %get-tuple-element.24), channel_id=1, source_target_pairs={{0,128},{128,0},{1,129},{129,1},{2,130},{130,2},{3,131},{131,3},{4... | collective-permute-start | bytes 7077896 | tf_op jit(solution)/shard_map/ppermute | solution.py:517
where the time goes:
time: 120 us
  starting transfers between devices  48.2 us (40%)
  Pallas kernels  30.8 us (26%)
  blocking collectives  18.5 us (15%)
  waiting for transfers between devices  16 us (13%)
  local copies, waits for them, and re-layouts  5.49 us (5%)
    ppermute x11, starting transfers between devices, along(): return lax.ppermute(array, ('band', 'grow'), pairs)  27 us
    all_to_all x1, blocking collectives, exchange(): col = lax.all_to_all(col, ('gcol_0', 'gcol_1'), 0, 0, tiled=True)  18.5 us
    ppermute x5, starting transfers between devices, swap(): return lax.ppermute(array, 'band', [(0, 1), (1, 0)])  12.2 us
    pallas_call x1, Pallas kernels, density_call(): pl.pallas_call(density_kernel, out_shape=[jax.ShapeDtypeStruct((N1, BLOCK...  12 us
    ppermute x11, waiting for transfers between devices, along(): return lax.ppermute(array, ('band', 'grow'), pairs)  9.1 us
    ppermute x7, starting transfers between devices, turned(): return lax.ppermute(array, PLANE, pairs)  8.92 us
    ppermute x7, waiting for transfers between devices, turned(): return lax.ppermute(array, PLANE, pairs)  5.58 us
    unnamed x6, local copies, waits for them, and re-layouts  5.43 us
  transfers between devices with their start and end apart: 23, of which 9 were waited for; matrix products, arithmetic and copies ran while one was open for 0% of the time, Pallas kernels for 8%

commit v1 on v0

--- a/solution.py
+++ b/solution.py
@@ -147,7 +147,7 @@
                 lhs[top : top + M1, where] = made.astype(BF16)
                 return carry
 
-            lax.fori_loop(0, CHUNKS, product, 0, unroll=6)
+            lax.fori_loop(0, CHUNKS, product, 0, unroll=12)
         gaps.append(gap)
 
     acc[...] = jnp.zeros_like(acc)
@@ -437,57 +437,28 @@
     )(weighted, early, above, far_a, far_b)
 
 
-def home_kernel(weighted, early, home_out):
+def home_kernel(weighted, early, late, home_out):
     def product(m, carry):
         where = pl.ds(pl.multiple_of(m * 256, 256), 256)
         home_out[where, :] = jnp.dot(
             early[where, :], weighted[:EARLY, :], preferred_element_type=F32
-        )
+        ) + jnp.dot(late[where, :], weighted[EARLY:, :], preferred_element_type=F32)
         return carry
 
     lax.fori_loop(0, ROW // 256, product, 0)
 
 
-def home_call(weighted, early, interpret=False):
+def home_call(weighted, early, late, interpret=False):
     vmem = pl.BlockSpec(memory_space=VMEM)
     return pl.pallas_call(
         home_kernel,
         out_shape=jax.ShapeDtypeStruct((ROW, NP), F32),
-        in_specs=[vmem] * 2,
+        in_specs=[vmem] * 3,
         out_specs=vmem,
         compiler_params=pltpu.CompilerParams(vmem_limit_bytes=16 << 20),
         interpret=interpret,
         name="home",
-    )(weighted, early)
-
-
-def finish_kernel(weighted, home, late, received, out, buffers, sems):
-    copies = []
-    for m in range(ROW // 256):
-        where = slice(m * 256, (m + 1) * 256)
-        slot = m % 2
-        if m >= 2:
-            copies[m - 2].wait()
-        made = jnp.dot(late[where, :], weighted[EARLY:, :], preferred_element_type=F32)
-        buffers[slot] = -(home[where, :] + made + received[where, :].astype(F32))
-        copies.append(pltpu.make_async_copy(buffers.at[slot], out.at[0, pl.ds(m * 256, 256), :], sems.at[m]))
-        copies[m].start()
-    copies[-2].wait()
-    copies[-1].wait()
-
-
-def finish_call(weighted, home, late, received, interpret=False):
-    vmem = pl.BlockSpec(memory_space=VMEM)
-    return pl.pallas_call(
-        finish_kernel,
-        out_shape=jax.ShapeDtypeStruct((1, ROW, NP), F32),
-        in_specs=[vmem] * 4,
-        out_specs=pl.BlockSpec(memory_space=pltpu.HBM),
-        scratch_shapes=[VMEM((2, 256, NP), F32), pltpu.SemaphoreType.DMA((ROW // 256,))],
-        compiler_params=pltpu.CompilerParams(vmem_limit_bytes=16 << 20),
-        interpret=interpret,
-        name="finish",
-    )(weighted, home, late, received)
+    )(weighted, early, late)
 
 
 PLANE = ("band", "gcol_0", "gcol_1")
@@ -559,8 +530,8 @@
     early = flip_call(line, below, above)
     away, late = away_call(weighted_away, early, above, far_a, far_b)
     received = swap(away)
-    home = home_call(weighted_home, early)
-    return finish_call(weighted_home, home, late, received)
+    home = home_call(weighted_home, early, late)
+    return -(home + received.astype(F32))[None]
 
 
 def solution(mesh):

time: 120 us -> 118 us (0.983)
  Pallas kernels: 30.8 us -> 27.4 us
  other arithmetic: 0.06 us -> 2.71 us
  waiting for transfers between devices: 16 us -> 14.7 us
    pallas_call x1 -> x0, Pallas kernels: 4.46 us -> none  [finish_call(): pl.pallas_call(finish_kernel, out_shape=jax.ShapeDtypeStruct((1, ROW, NP)...]
    neg x0 -> x1, other arithmetic: none -> 2.64 us  [exchange(): return -(home + received.astype(F32))[None]]
    ppermute x5, waiting for transfers between devices: 1.29 us -> 0.05 us  [swap(): return lax.ppermute(array, 'band', [(0, 1), (1, 0)])]
    pallas_call x1, Pallas kernels: 2.87 us -> 4.11 us  [home_call(): pl.pallas_call(home_kernel, out_shape=jax.ShapeDtypeStruct((ROW, NP), F32...]
  transfers between devices with their start and end apart: 23 -> 23, of which waited for: 9 -> 7; matrix products, arithmetic and copies ran while one was open for 0% -> 0% of each run, Pallas kernels for 8% -> 9%
where the time goes in v1:
time: 118 us
  starting transfers between devices  48.2 us (41%)
  Pallas kernels  27.4 us (23%)
  blocking collectives  18.5 us (16%)
  waiting for transfers between devices  14.7 us (12%)
  local copies, waits for them, and re-layouts  5.49 us (5%)
  other arithmetic  2.71 us (2%)
    ppermute x11, starting transfers between devices, along(): return lax.ppermute(array, ('band', 'grow'), pairs)  27 us
    all_to_all x1, blocking collectives, exchange(): col = lax.all_to_all(col, ('gcol_0', 'gcol_1'), 0, 0, tiled=True)  18.5 us
    ppermute x5, starting transfers between devices, swap(): return lax.ppermute(array, 'band', [(0, 1), (1, 0)])  12.3 us
    pallas_call x1, Pallas kernels, density_call(): pl.pallas_call(density_kernel, out_shape=[jax.ShapeDtypeStruct((N1, BLOCK...  11.9 us
    ppermute x11, waiting for transfers between devices, along(): return lax.ppermute(array, ('band', 'grow'), pairs)  9.09 us
    ppermute x7, starting transfers between devices, turned(): return lax.ppermute(array, PLANE, pairs)  8.94 us
    ppermute x7, waiting for transfers between devices, turned(): return lax.ppermute(array, PLANE, pairs)  5.57 us
    unnamed x6, local copies, waits for them, and re-layouts  5.43 us
  transfers between devices with their start and end apart: 23, of which 7 were waited for; matrix products, arithmetic and copies ran while one was open for 0% of the time, Pallas kernels for 9%

profile of v1, /device:TPU:1, one launch (start us, length us, event | category | flops | bytes accessed | tf_op | source)
XLA Modules:
  0.0 117.8 jit_solution(16880361856587570794)
XLA Ops:
  0.0 3.2 %collective-permute-start.2 = (bf16[4,98304]{1,0:T(4,128)(2,1)}, bf16[4,98304]{1,0:T(4,128)(2,1)S(1)}, u32[]{:S(2)}, u32[]{:S(2)}) collective-permute-start(bf16[4,98304]{1,0:T(4,128)(2,1)} %refs_0_.1), channel_id=1, source_target_pairs={{0,128},{128,0},{1,129},{129,1},{2,130},{130,2},{3,131},{131,3},{4... | collective-permute-start | bytes 2359304 | tf_op jit(solution)/shard_map/ppermute | solution.py:488
  3.2 0.0 collective-permute-start.1
  3.2 0.5 collective-permute-start
  4.4 0.0 copy-start.2
  4.4 2.1 %ready.1.vals = f32[12352,128]{1,0:T(8,128)S(1)} custom-call(bf16[16,98304]{1,0:T(8,128)(2,1)} %source.1), custom_call_target="tpu_custom_call" | custom-call | tf_op jit(solution)/shard_map/ready/pallas_call | solution.py:83
  6.5 0.0 copy-start
  6.5 2.6 %copy-done = f32[12352,128]{1,0:T(8,128)} copy-done((f32[12352,128]{1,0:T(8,128)}, f32[12352,128]{1,0:T(8,128)S(1)}, u32[]{:S(2)}) %copy-start) | copy-done | bytes 6324248
  9.2 0.0 collective-permute-done.1.other_count
  9.2 0.0 collective-permute-done.other
  9.2 0.0 collective-permute-done.2.refs_1_
  9.2 0.0 copy-done.2
  9.2 0.0 copy-start.1
  9.2 2.8 %copy-done.1 = f32[12352,128]{1,0:T(8,128)S(1)} copy-done((f32[12352,128]{1,0:T(8,128)S(1)}, f32[12352,128]{1,0:T(8,128)}, u32[]{:S(2)}) %copy-start.1) | copy-done | bytes 6324248
  12.0 11.9 %density.1 = (bf16[16,64,128]{2,1,0:T(8,128)(2,1)S(1)}, bf16[1,120,128]{2,1,0:T(8,128)(2,1)S(1)}, bf16[2,120,128]{2,1,0:T(8,128)(2,1)S(1)}, bf16[2,120,128]{2,1,...) custom-call(s32[1]{0:T(128)} %bitcast.place, s32[2,20]{1,0:T(2,128)S(1)} %copy-done.2, ...), custom_call_target="tpu_custom_call" | custom-call | tf_op jit(solution)/shard_map/density/pallas_call | solution.py:244
  23.9 3.9 %collective-permute-start.11 = (bf16[2,120,128]{2,1,0:T(8,128)(2,1)S(1)}, bf16[2,120,128]{2,1,0:T(8,128)(2,1)S(1)}, u32[]{:S(2)}, u32[]{:S(2)}) collective-permute-start(bf16[2,120,128]{2,1,0:T(8,128)(2,1)S(1)} %get-tuple-element.18), channel_id=1, source_target_pairs={{0,16},{16,32},{32,48},{48,64},{64,80},{80,96},{96,112},{112,0},{1... | collective-permute-start | bytes 184328 | tf_op jit(solution)/shard_map/ppermute | solution.py:484
  27.8 1.1 collective-permute-start.12
  28.9 0.5 collective-permute-start.13
  29.4 4.4 %collective-permute-start.14 = (bf16[1,120,128]{2,1,0:T(8,128)(2,1)S(1)}, bf16[1,120,128]{2,1,0:T(8,128)(2,1)S(1)}, u32[]{:S(2)}, u32[]{:S(2)}) collective-permute-start(bf16[1,120,128]{2,1,0:T(8,128)(2,1)S(1)} %get-tuple-element.21), channel_id=1, source_target_pairs={{0,64},{16,80},{32,96},{48,112},{64,0},{80,16},{96,32},{112,48},{1... | collective-permute-start | bytes 92168 | tf_op jit(solution)/shard_map/ppermute | solution.py:484
  33.9 3.5 %collective-permute-done.14.refs_4_ = bf16[1,120,128]{2,1,0:T(8,128)(2,1)S(1)} collective-permute-done((bf16[1,120,128]{2,1,0:T(8,128)(2,1)S(1)}, bf16[1,120,128]{2,1,0:T(8,128)(2,1)S(1)}, u32[]{:S(2)}, u32[]{:S(2)}) %collective-permute-start.14) | collective-permute-done | bytes 30752 | tf_op jit(solution)/shard_map/ppermute | solution.py:484
  37.4 0.0 collective-permute-done.11.refs_1_
  37.4 0.0 collective-permute-done.12.refs_2_
  37.4 0.0 collective-permute-done.13.refs_3_
  37.4 0.1 pack.1
  37.5 3.0 %collective-permute-start.17 = (bf16[80,1536]{1,0:T(8,128)(2,1)S(1)}, bf16[80,1536]{1,0:T(8,128)(2,1)S(1)}, u32[]{:S(2)}, u32[]{:S(2)}) collective-permute-start(bf16[80,1536]{1,0:T(8,128)(2,1)S(1)} %pack.1), channel_id=1, source_target_pairs={{0,2},{1,3},{2,0},{3,1},{4,6},{5,7},{6,4},{7,5},{8,10},{9,11},{10,... | collective-permute-start | bytes 737288 | tf_op jit(solution)/shard_map/ppermute | solution.py:475
  40.5 0.8 collective-permute-start.16
  41.3 0.7 collective-permute-start.15
  42.0 2.4 %collective-permute-done.17 = bf16[80,1536]{1,0:T(8,128)(2,1)S(1)} collective-permute-done((bf16[80,1536]{1,0:T(8,128)(2,1)S(1)}, bf16[80,1536]{1,0:T(8,128)(2,1)S(1)}, u32[]{:S(2)}, u32[]{:S(2)}) %collective-permute-start.17) | collective-permute-done | bytes 245792 | tf_op jit(solution)/shard_map/ppermute | solution.py:475
  44.4 3.1 %collective-permute-done.16 = bf16[80,1536]{1,0:T(8,128)(2,1)S(1)} collective-permute-done((bf16[80,1536]{1,0:T(8,128)(2,1)S(1)}, bf16[80,1536]{1,0:T(8,128)(2,1)S(1)}, u32[]{:S(2)}, u32[]{:S(2)}) %collective-permute-start.16) | collective-permute-done | bytes 245792 | tf_op jit(solution)/shard_map/ppermute | solution.py:475
  47.5 0.0 collective-permute-done.15
  47.6 0.1 pad_maximum_fusion.line
  47.6 2.8 %collective-permute-start.19 = (bf16[320,1536]{1,0:T(8,128)(2,1)S(1)}, bf16[320,1536]{1,0:T(8,128)(2,1)S(1)}, u32[]{:S(2)}, u32[]{:S(2)}) collective-permute-start(bf16[320,1536]{1,0:T(8,128)(2,1)S(1)} %pad_maximum_fusion.line), channel_id=1, source_target_pairs={{0,12},{1,13},{2,14},{3,15},{4,0},{5,1},{6,2},{7,3},{8,4},{9,5},{1... | collective-permute-start | bytes 2949128 | tf_op jit(solution)/shard_map/ppermute | solution.py:475
  50.5 0.0 collective-permute-start.18
  50.5 18.5 %all_to_all.5 = bf16[16,64,128]{2,1,0:T(8,128)(2,1)S(1)} all-to-all(bf16[16,64,128]{2,1,0:T(8,128)(2,1)S(1)} %get-tuple-element.15), channel_id=1, replica_groups=mesh['band'=2,'grow'=8,'gcol_0'=4,'gcol_1'=4] {'gcol_0','gcol_1'}, dimensions={0} | all-to-all | bytes 524288 | tf_op jit(solution)/shard_map/all_to_all | solution.py:513
  68.9 3.4 %collective-permute-start.4 = (bf16[16,64,128]{2,1,0:T(8,128)(2,1)S(1)}, bf16[16,64,128]{2,1,0:T(8,128)(2,1)S(1)}, u32[]{:S(2)}, u32[]{:S(2)}) collective-permute-start(bf16[16,64,128]{2,1,0:T(8,128)(2,1)S(1)} %all_to_all.5), channel_id=1, source_target_pairs={{0,128},{128,0},{1,129},{129,1},{2,130},{130,2},{3,131},{131,3},{4... | collective-permute-start | bytes 786440 | tf_op jit(solution)/shard_map/ppermute | solution.py:488
  72.3 2.6 %collective-permute-start.3 = (bf16[16,64,128]{2,1,0:T(8,128)(2,1)S(1)}, bf16[16,64,128]{2,1,0:T(8,128)(2,1)S(1)}, u32[]{:S(2)}, u32[]{:S(2)}) collective-permute-start(bf16[16,64,128]{2,1,0:T(8,128)(2,1)S(1)} %all_to_all.5), channel_id=1, source_target_pairs={{0,16},{16,32},{32,48},{48,64},{64,80},{80,96},{96,112},{112,0},{1... | collective-permute-start | bytes 786440 | tf_op jit(solution)/shard_map/ppermute | solution.py:484
  74.9 0.0 collective-permute-done.4.refs_1_
  74.9 1.2 collective-permute-start.6
  76.1 2.2 %collective-permute-done.3.refs_0_ = bf16[16,64,128]{2,1,0:T(8,128)(2,1)S(1)} collective-permute-done((bf16[16,64,128]{2,1,0:T(8,128)(2,1)S(1)}, bf16[16,64,128]{2,1,0:T(8,128)(2,1)S(1)}, u32[]{:S(2)}, u32[]{:S(2)}) %collective-permute-start.3) | collective-permute-done | bytes 262176 | tf_op jit(solution)/shard_map/ppermute | solution.py:484
  78.2 3.1 %collective-permute-start.5 = (bf16[16,64,128]{2,1,0:T(8,128)(2,1)S(1)}, bf16[16,64,128]{2,1,0:T(8,128)(2,1)S(1)}, u32[]{:S(2)}, u32[]{:S(2)}) collective-permute-start(bf16[16,64,128]{2,1,0:T(8,128)(2,1)S(1)} %collective-permute-done.3.refs_0_), channel_id=1, source_target_pairs={{0,16},{16,32},{32,48},{48,64},{64,80},{80,96},{96,112},{112,0},{1... | collective-permute-start | bytes 786440 | tf_op jit(solution)/shard_map/ppermute | solution.py:484
  81.3 0.0 collective-permute-done.6.refs_3_
  81.3 2.8 %collective-permute-start.8 = (bf16[16,64,128]{2,1,0:T(8,128)(2,1)S(1)}, bf16[16,64,128]{2,1,0:T(8,128)(2,1)S(1)}, u32[]{:S(2)}, u32[]{:S(2)}) collective-permute-start(bf16[16,64,128]{2,1,0:T(8,128)(2,1)S(1)} %collective-permute-done.6.refs_3_), channel_id=1, source_target_pairs={{0,16},{16,32},{32,48},{48,64},{64,80},{80,96},{96,112},{112,0},{1... | collective-permute-start | bytes 786440 | tf_op jit(solution)/shard_map/ppermute | solution.py:484
  84.1 0.5 collective-permute-done.5.refs_2_
  84.6 3.1 %collective-permute-start.7 = (bf16[16,64,128]{2,1,0:T(8,128)(2,1)S(1)}, bf16[16,64,128]{2,1,0:T(8,128)(2,1)S(1)}, u32[]{:S(2)}, u32[]{:S(2)}) collective-permute-start(bf16[16,64,128]{2,1,0:T(8,128)(2,1)S(1)} %collective-permute-done.5.refs_2_), channel_id=1, source_target_pairs={{0,16},{16,32},{32,48},{48,64},{64,80},{80,96},{96,112},{112,0},{1... | collective-permute-start | bytes 786440 | tf_op jit(solution)/shard_map/ppermute | solution.py:484
  87.8 0.0 collective-permute-done.19.above
  87.8 1.3 %collective-permute-start.21 = (bf16[160,1536]{1,0:T(8,128)(2,1)S(1)}, bf16[160,1536]{1,0:T(8,128)(2,1)S(1)}, u32[]{:S(2)}, u32[]{:S(2)}) collective-permute-start(bf16[160,1536]{1,0:T(8,128)(2,1)S(1)} %slice.9), channel_id=1, source_target_pairs={{0,12},{1,13},{2,14},{3,15},{4,0},{5,1},{6,2},{7,3},{8,4},{9,5},{1... | collective-permute-start | bytes 1474568 | tf_op jit(solution)/shard_map/ppermute | solution.py:475
  89.1 0.0 collective-permute-done.18.below
  89.1 0.3 collective-permute-start.20
  89.5 0.0 collective-permute-done.8.refs_5_
  89.5 1.1 collective-permute-start.10
  90.6 0.5 collective-permute-done.7.refs_4_
  91.1 3.1 %collective-permute-start.9 = (bf16[16,64,128]{2,1,0:T(8,128)(2,1)S(1)}, bf16[16,64,128]{2,1,0:T(8,128)(2,1)S(1)}, u32[]{:S(2)}, u32[]{:S(2)}) collective-permute-start(bf16[16,64,128]{2,1,0:T(8,128)(2,1)S(1)} %collective-permute-done.7.refs_4_), channel_id=1, source_target_pairs={{0,16},{16,32},{32,48},{48,64},{64,80},{80,96},{96,112},{112,0},{1... | collective-permute-start | bytes 786440 | tf_op jit(solution)/shard_map/ppermute | solution.py:484
  94.2 0.9 flip.1.early
  95.1 0.0 collective-permute-done.10.refs_7_
  95.1 2.4 %collective-permute-done.9.refs_6_ = bf16[16,64,128]{2,1,0:T(8,128)(2,1)S(1)} collective-permute-done((bf16[16,64,128]{2,1,0:T(8,128)(2,1)S(1)}, bf16[16,64,128]{2,1,0:T(8,128)(2,1)S(1)}, u32[]{:S(2)}, u32[]{:S(2)}) %collective-permute-start.9) | collective-permute-done | bytes 262176 | tf_op jit(solution)/shard_map/ppermute | solution.py:484
  97.5 3.2 %assemble.1 = (bf16[1280,768]{1,0:T(8,128)(2,1)S(1)}, bf16[1280,768]{1,0:T(8,128)(2,1)S(1)}) custom-call(s32[1]{0:T(128)} %bitcast.place, bf16[16,64,128]{2,1,0:T(8,128)(2,1)S(1)} %collective-permute-done.3.refs_0_, bf16[16,64,128]{2,1,0:T(8,128)(2,1)S(1)} %collective-permute-done.4.refs_1_, bf16[16,64,128]{2,1,0:T(8,128)(2,1)S(1)} %collective-permute-done.5.refs_2_, ...), custom_call_target="tpu_custom_call" | custom-call | tf_op jit(solution)/shard_map/assemble/pallas_call | solution.py:356
  100.7 0.0 collective-permute-done.21.far_b
  100.7 0.0 collective-permute-done.20.far_a
  100.7 5.0 %away.1 = (bf16[1536,768]{1,0:T(8,128)(2,1)S(1)}, bf16[1536,512]{1,0:T(8,128)(2,1)S(1)}) custom-call(bf16[1280,768]{1,0:T(8,128)(2,1)S(1)} %get-tuple-element.22.weighted, bf16[1536,768]{1,0:T(8,128)(2,1)S(1)} %flip.1.early, bf16[320,1536]{1,0:T(8,128)(2,1)S(1)} %collective-permute-done.19.above, bf16[160,1536]{1,0:T(8,128)(2,1)S(1)} %collective-permute-done.20.far_a, ...), custom_call_target="tpu_custom_call" | custom-call | tf_op jit(solution)/shard_map/away/pallas_call | solution.py:425
  105.8 5.2 %collective-permute-start.22 = (bf16[1536,768]{1,0:T(8,128)(2,1)S(1)}, bf16[1536,768]{1,0:T(8,128)(2,1)S(1)}, u32[]{:S(2)}, u32[]{:S(2)}) collective-permute-start(bf16[1536,768]{1,0:T(8,128)(2,1)S(1)} %get-tuple-element.24), channel_id=1, source_target_pairs={{0,128},{128,0},{1,129},{129,1},{2,130},{130,2},{3,131},{131,3},{4... | collective-permute-start | bytes 7077896 | tf_op jit(solution)/shard_map/ppermute | solution.py:488
  111.0 4.1 %home.1 = f32[1536,768]{1,0:T(8,128)S(1)} custom-call(bf16[1280,768]{1,0:T(8,128)(2,1)S(1)} %get-tuple-element.16.weighted, bf16[1536,768]{1,0:T(8,128)(2,1)S(1)} %flip.1.early, bf16[1536,512]{1,0:T(8,128)(2,1)S(1)} %get-tuple-element.23.late), custom_call_target="tpu_custom_call" | custom-call | tf_op jit(solution)/shard_map/home/pallas_call | solution.py:453
  115.1 0.0 collective-permute-done.22
  115.2 2.6 %negate_bitcast_fusion = f32[1,1536,768]{2,1,0:T(8,128)} fusion(f32[1536,768]{1,0:T(8,128)S(1)} %home.1, bf16[1536,768]{1,0:T(8,128)(2,1)S(1)} %collective-permute-done.22), kind=kLoop, calls=%fused_computation | loop fusion | flops 3538944 | bytes 11796480 | tf_op jit(solution)/shard_map/neg | solution.py:534
  (2 shorter events, 0.1 us)
Async XLA Ops:
  0.0 9.2 %collective-permute-start.2 = (bf16[4,98304]{1,0:T(4,128)(2,1)}, bf16[4,98304]{1,0:T(4,128)(2,1)S(1)}, u32[]{:S(2)}, u32[]{:S(2)}) collective-permute-start(bf16[4,98304]{1,0:T(4,128)(2,1)} %refs_0_.1), channel_id=1, source_target_pairs={{0,128},{128,0},{1,129},{129,1},{2,130},{130,2},{3,131},{131,3},{4... | collective-permute-start | bytes 2359304 | tf_op jit(solution)/shard_map/ppermute | solution.py:488
  3.2 6.0 %collective-permute-start.1 = (s32[1]{0:T(128)}, s32[1]{0:T(128)}, u32[]{:S(2)}, u32[]{:S(2)}) collective-permute-start(s32[1]{0:T(128)} %param.17), channel_id=1, source_target_pairs={{0,128},{128,0},{1,129},{129,1},{2,130},{130,2},{3,131},{131,3},{4... | collective-permute-start | bytes 20 | tf_op jit(solution)/shard_map/ppermute | solution.py:488
  3.2 6.0 %collective-permute-start = (s32[2,20]{1,0:T(2,128)}, s32[2,20]{1,0:T(2,128)S(1)}, u32[]{:S(2)}, u32[]{:S(2)}) collective-permute-start(s32[2,20]{1,0:T(2,128)} %mine.1), channel_id=1, source_target_pairs={{0,128},{128,0},{1,129},{129,1},{2,130},{130,2},{3,131},{131,3},{4... | collective-permute-start | bytes 488 | tf_op jit(solution)/shard_map/ppermute | solution.py:488
  4.4 4.8 %copy-start.2 = (s32[2,20]{1,0:T(2,128)S(1)}, s32[2,20]{1,0:T(2,128)}, u32[]{:S(2)}) copy-start(s32[2,20]{1,0:T(2,128)} %mine.1) | copy-start | bytes 484
  6.5 2.6 %copy-start = (f32[12352,128]{1,0:T(8,128)}, f32[12352,128]{1,0:T(8,128)S(1)}, u32[]{:S(2)}) copy-start(f32[12352,128]{1,0:T(8,128)S(1)} %ready.1.vals) | copy-start | bytes 18972676
  9.2 2.8 %copy-start.1 = (f32[12352,128]{1,0:T(8,128)S(1)}, f32[12352,128]{1,0:T(8,128)}, u32[]{:S(2)}) copy-start(f32[12352,128]{1,0:T(8,128)} %copy-done) | copy-start | bytes 18972676
  23.9 13.5 %collective-permute-start.11 = (bf16[2,120,128]{2,1,0:T(8,128)(2,1)S(1)}, bf16[2,120,128]{2,1,0:T(8,128)(2,1)S(1)}, u32[]{:S(2)}, u32[]{:S(2)}) collective-permute-start(bf16[2,120,128]{2,1,0:T(8,128)(2,1)S(1)} %get-tuple-element.18), channel_id=1, source_target_pairs={{0,16},{16,32},{32,48},{48,64},{64,80},{80,96},{96,112},{112,0},{1... | collective-permute-start | bytes 184328 | tf_op jit(solution)/shard_map/ppermute | solution.py:484
  27.8 9.6 %collective-permute-start.12 = (bf16[2,120,128]{2,1,0:T(8,128)(2,1)S(1)}, bf16[2,120,128]{2,1,0:T(8,128)(2,1)S(1)}, u32[]{:S(2)}, u32[]{:S(2)}) collective-permute-start(bf16[2,120,128]{2,1,0:T(8,128)(2,1)S(1)} %get-tuple-element.19), channel_id=1, source_target_pairs={{0,32},{16,48},{32,64},{48,80},{64,96},{80,112},{96,0},{112,16},{1... | collective-permute-start | bytes 184328 | tf_op jit(solution)/shard_map/ppermute | solution.py:484
  28.9 8.5 %collective-permute-start.13 = (bf16[2,120,128]{2,1,0:T(8,128)(2,1)S(1)}, bf16[2,120,128]{2,1,0:T(8,128)(2,1)S(1)}, u32[]{:S(2)}, u32[]{:S(2)}) collective-permute-start(bf16[2,120,128]{2,1,0:T(8,128)(2,1)S(1)} %get-tuple-element.20), channel_id=1, source_target_pairs={{0,48},{16,64},{32,80},{48,96},{64,112},{80,0},{96,16},{112,32},{1... | collective-permute-start | bytes 184328 | tf_op jit(solution)/shard_map/ppermute | solution.py:484
  29.4 8.0 %collective-permute-start.14 = (bf16[1,120,128]{2,1,0:T(8,128)(2,1)S(1)}, bf16[1,120,128]{2,1,0:T(8,128)(2,1)S(1)}, u32[]{:S(2)}, u32[]{:S(2)}) collective-permute-start(bf16[1,120,128]{2,1,0:T(8,128)(2,1)S(1)} %get-tuple-element.21), channel_id=1, source_target_pairs={{0,64},{16,80},{32,96},{48,112},{64,0},{80,16},{96,32},{112,48},{1... | collective-permute-start | bytes 92168 | tf_op jit(solution)/shard_map/ppermute | solution.py:484
  37.5 6.9 %collective-permute-start.17 = (bf16[80,1536]{1,0:T(8,128)(2,1)S(1)}, bf16[80,1536]{1,0:T(8,128)(2,1)S(1)}, u32[]{:S(2)}, u32[]{:S(2)}) collective-permute-start(bf16[80,1536]{1,0:T(8,128)(2,1)S(1)} %pack.1), channel_id=1, source_target_pairs={{0,2},{1,3},{2,0},{3,1},{4,6},{5,7},{6,4},{7,5},{8,10},{9,11},{10,... | collective-permute-start | bytes 737288 | tf_op jit(solution)/shard_map/ppermute | solution.py:475
  40.5 7.0 %collective-permute-start.16 = (bf16[80,1536]{1,0:T(8,128)(2,1)S(1)}, bf16[80,1536]{1,0:T(8,128)(2,1)S(1)}, u32[]{:S(2)}, u32[]{:S(2)}) collective-permute-start(bf16[80,1536]{1,0:T(8,128)(2,1)S(1)} %pack.1), channel_id=1, source_target_pairs={{0,3},{1,0},{2,1},{3,2},{4,7},{5,4},{6,5},{7,6},{8,11},{9,8},{10,9... | collective-permute-start | bytes 737288 | tf_op jit(solution)/shard_map/ppermute | solution.py:475
  41.3 6.3 %collective-permute-start.15 = (bf16[80,1536]{1,0:T(8,128)(2,1)S(1)}, bf16[80,1536]{1,0:T(8,128)(2,1)S(1)}, u32[]{:S(2)}, u32[]{:S(2)}) collective-permute-start(bf16[80,1536]{1,0:T(8,128)(2,1)S(1)} %pack.1), channel_id=1, source_target_pairs={{0,1},{1,2},{2,3},{3,0},{4,5},{5,6},{6,7},{7,4},{8,9},{9,10},{10,1... | collective-permute-start | bytes 737288 | tf_op jit(solution)/shard_map/ppermute | solution.py:475
  47.6 40.1 %collective-permute-start.19 = (bf16[320,1536]{1,0:T(8,128)(2,1)S(1)}, bf16[320,1536]{1,0:T(8,128)(2,1)S(1)}, u32[]{:S(2)}, u32[]{:S(2)}) collective-permute-start(bf16[320,1536]{1,0:T(8,128)(2,1)S(1)} %pad_maximum_fusion.line), channel_id=1, source_target_pairs={{0,12},{1,13},{2,14},{3,15},{4,0},{5,1},{6,2},{7,3},{8,4},{9,5},{1... | collective-permute-start | bytes 2949128 | tf_op jit(solution)/shard_map/ppermute | solution.py:475
  50.5 38.7 %collective-permute-start.18 = (bf16[320,1536]{1,0:T(8,128)(2,1)S(1)}, bf16[320,1536]{1,0:T(8,128)(2,1)S(1)}, u32[]{:S(2)}, u32[]{:S(2)}) collective-permute-start(bf16[320,1536]{1,0:T(8,128)(2,1)S(1)} %pad_maximum_fusion.line), channel_id=1, source_target_pairs={{0,4},{1,5},{2,6},{3,7},{4,8},{5,9},{6,10},{7,11},{8,12},{9,13},{1... | collective-permute-start | bytes 2949128 | tf_op jit(solution)/shard_map/ppermute | solution.py:475
  68.9 6.0 %collective-permute-start.4 = (bf16[16,64,128]{2,1,0:T(8,128)(2,1)S(1)}, bf16[16,64,128]{2,1,0:T(8,128)(2,1)S(1)}, u32[]{:S(2)}, u32[]{:S(2)}) collective-permute-start(bf16[16,64,128]{2,1,0:T(8,128)(2,1)S(1)} %all_to_all.5), channel_id=1, source_target_pairs={{0,128},{128,0},{1,129},{129,1},{2,130},{130,2},{3,131},{131,3},{4... | collective-permute-start | bytes 786440 | tf_op jit(solution)/shard_map/ppermute | solution.py:488
  72.3 5.9 %collective-permute-start.3 = (bf16[16,64,128]{2,1,0:T(8,128)(2,1)S(1)}, bf16[16,64,128]{2,1,0:T(8,128)(2,1)S(1)}, u32[]{:S(2)}, u32[]{:S(2)}) collective-permute-start(bf16[16,64,128]{2,1,0:T(8,128)(2,1)S(1)} %all_to_all.5), channel_id=1, source_target_pairs={{0,16},{16,32},{32,48},{48,64},{64,80},{80,96},{96,112},{112,0},{1... | collective-permute-start | bytes 786440 | tf_op jit(solution)/shard_map/ppermute | solution.py:484
  74.9 6.4 %collective-permute-start.6 = (bf16[16,64,128]{2,1,0:T(8,128)(2,1)S(1)}, bf16[16,64,128]{2,1,0:T(8,128)(2,1)S(1)}, u32[]{:S(2)}, u32[]{:S(2)}) collective-permute-start(bf16[16,64,128]{2,1,0:T(8,128)(2,1)S(1)} %collective-permute-done.4.refs_1_), channel_id=1, source_target_pairs={{0,16},{16,32},{32,48},{48,64},{64,80},{80,96},{96,112},{112,0},{1... | collective-permute-start | bytes 786440 | tf_op jit(solution)/shard_map/ppermute | solution.py:484
  78.2 6.4 %collective-permute-start.5 = (bf16[16,64,128]{2,1,0:T(8,128)(2,1)S(1)}, bf16[16,64,128]{2,1,0:T(8,128)(2,1)S(1)}, u32[]{:S(2)}, u32[]{:S(2)}) collective-permute-start(bf16[16,64,128]{2,1,0:T(8,128)(2,1)S(1)} %collective-permute-done.3.refs_0_), channel_id=1, source_target_pairs={{0,16},{16,32},{32,48},{48,64},{64,80},{80,96},{96,112},{112,0},{1... | collective-permute-start | bytes 786440 | tf_op jit(solution)/shard_map/ppermute | solution.py:484
  81.3 8.1 %collective-permute-start.8 = (bf16[16,64,128]{2,1,0:T(8,128)(2,1)S(1)}, bf16[16,64,128]{2,1,0:T(8,128)(2,1)S(1)}, u32[]{:S(2)}, u32[]{:S(2)}) collective-permute-start(bf16[16,64,128]{2,1,0:T(8,128)(2,1)S(1)} %collective-permute-done.6.refs_3_), channel_id=1, source_target_pairs={{0,16},{16,32},{32,48},{48,64},{64,80},{80,96},{96,112},{112,0},{1... | collective-permute-start | bytes 786440 | tf_op jit(solution)/shard_map/ppermute | solution.py:484
  84.6 6.4 %collective-permute-start.7 = (bf16[16,64,128]{2,1,0:T(8,128)(2,1)S(1)}, bf16[16,64,128]{2,1,0:T(8,128)(2,1)S(1)}, u32[]{:S(2)}, u32[]{:S(2)}) collective-permute-start(bf16[16,64,128]{2,1,0:T(8,128)(2,1)S(1)} %collective-permute-done.5.refs_2_), channel_id=1, source_target_pairs={{0,16},{16,32},{32,48},{48,64},{64,80},{80,96},{96,112},{112,0},{1... | collective-permute-start | bytes 786440 | tf_op jit(solution)/shard_map/ppermute | solution.py:484
  87.8 12.9 %collective-permute-start.21 = (bf16[160,1536]{1,0:T(8,128)(2,1)S(1)}, bf16[160,1536]{1,0:T(8,128)(2,1)S(1)}, u32[]{:S(2)}, u32[]{:S(2)}) collective-permute-start(bf16[160,1536]{1,0:T(8,128)(2,1)S(1)} %slice.9), channel_id=1, source_target_pairs={{0,12},{1,13},{2,14},{3,15},{4,0},{5,1},{6,2},{7,3},{8,4},{9,5},{1... | collective-permute-start | bytes 1474568 | tf_op jit(solution)/shard_map/ppermute | solution.py:475
  89.1 11.6 %collective-permute-start.20 = (bf16[160,1536]{1,0:T(8,128)(2,1)S(1)}, bf16[160,1536]{1,0:T(8,128)(2,1)S(1)}, u32[]{:S(2)}, u32[]{:S(2)}) collective-permute-start(bf16[160,1536]{1,0:T(8,128)(2,1)S(1)} %slice.8), channel_id=1, source_target_pairs={{0,4},{1,5},{2,6},{3,7},{4,8},{5,9},{6,10},{7,11},{8,12},{9,13},{1... | collective-permute-start | bytes 1474568 | tf_op jit(solution)/shard_map/ppermute | solution.py:475
  89.5 5.7 %collective-permute-start.10 = (bf16[16,64,128]{2,1,0:T(8,128)(2,1)S(1)}, bf16[16,64,128]{2,1,0:T(8,128)(2,1)S(1)}, u32[]{:S(2)}, u32[]{:S(2)}) collective-permute-start(bf16[16,64,128]{2,1,0:T(8,128)(2,1)S(1)} %collective-permute-done.8.refs_5_), channel_id=1, source_target_pairs={{0,16},{16,32},{32,48},{48,64},{64,80},{80,96},{96,112},{112,0},{1... | collective-permute-start | bytes 786440 | tf_op jit(solution)/shard_map/ppermute | solution.py:484
  91.1 6.4 %collective-permute-start.9 = (bf16[16,64,128]{2,1,0:T(8,128)(2,1)S(1)}, bf16[16,64,128]{2,1,0:T(8,128)(2,1)S(1)}, u32[]{:S(2)}, u32[]{:S(2)}) collective-permute-start(bf16[16,64,128]{2,1,0:T(8,128)(2,1)S(1)} %collective-permute-done.7.refs_4_), channel_id=1, source_target_pairs={{0,16},{16,32},{32,48},{48,64},{64,80},{80,96},{96,112},{112,0},{1... | collective-permute-start | bytes 786440 | tf_op jit(solution)/shard_map/ppermute | solution.py:484
  105.8 9.4 %collective-permute-start.22 = (bf16[1536,768]{1,0:T(8,128)(2,1)S(1)}, bf16[1536,768]{1,0:T(8,128)(2,1)S(1)}, u32[]{:S(2)}, u32[]{:S(2)}) collective-permute-start(bf16[1536,768]{1,0:T(8,128)(2,1)S(1)} %get-tuple-element.24), channel_id=1, source_target_pairs={{0,128},{128,0},{1,129},{129,1},{2,130},{130,2},{3,131},{131,3},{4... | collective-permute-start | bytes 7077896 | tf_op jit(solution)/shard_map/ppermute | solution.py:488
